TPU v7x, 128 devices: a whole 4x4x4 slice. The times are simulated.
128 devices in a mesh: pipe: 2 (over core), tensor: 2 (over x_lo), dp: 32 (over y, z, x_hi).
Axes of the slice: x: 4 (x_hi: 2, x_lo: 2; x = x_hi * 2 + x_lo), y: 4, z: 4, core: 2. Of those that a mesh axis runs over, the one named last changes fastest.
Arguments:
- section_in: bfloat16 [2, 32, 2, 128, 1024], P('pipe', 'dp', 'tensor'), may hold values from -12 to 12
- lengths: int32 [32, 2], P('dp'), may hold values from 32 to 128, as said below
- qkv_weight: bfloat16 [2, 3, 1024, 1024], P('pipe', None, None, 'tensor'), may hold values from -0.75 to 0.75
- qv_bias: bfloat16 [2, 2, 1024], P('pipe', None, 'tensor'), may hold values from -3 to 3
- out_weight: bfloat16 [2, 1024, 1024], P('pipe', 'tensor'), may hold values from -0.5 to 0.5
- up_weight: bfloat16 [2, 1024, 2048], P('pipe', None, 'tensor'), may hold values from -0.1875 to 0.1875
- up_bias: bfloat16 [2, 2048], P('pipe', 'tensor'), may hold values from -3 to 3
- down_weight: bfloat16 [2, 2048, 1024], P('pipe', 'tensor'), may hold values from -0.125 to 0.125
- norm_gains: float32 [2, 2, 1024], P('pipe'), may hold values from 0.5 to 1.5
- row_biases: float32 [2, 4, 1024], P('pipe'), may hold values from -2 to 2
Outputs:
- section_out: float32 [2, 32, 2, 128, 1024], P('pipe', 'dp', 'tensor')
- qkv_grad: float32 [2, 3, 1024, 1024], P('pipe', None, None, 'tensor')
- qv_bias_grad: float32 [2, 2, 1024], P('pipe', None, 'tensor')
- out_grad: float32 [2, 1024, 1024], P('pipe', 'tensor')
- up_grad: float32 [2, 1024, 2048], P('pipe', None, 'tensor')
- up_bias_grad: float32 [2, 2048], P('pipe', 'tensor')
- down_grad: float32 [2, 2048, 1024], P('pipe', 'tensor')
- gain_grad: float32 [2, 2, 1024], P('pipe')
- bias_grad: float32 [2, 4, 1024], P('pipe')
Inputs may be any that keep to these rules, and one draw needn't show every extreme that they name: `lengths`: some sequence has length exactly 128 and some exactly 32.
All inputs are finite; a program needn't handle non-finite values.
Results may differ from a plain program's by a relative error of at most 0.023.
Values may be sent and summed in bfloat16 or wider, within the bound.
No kernel may reach another device: no remote copies, remote signals or barrier semaphores. Data moves between devices by JAX's collectives and lax.ppermute only.
A program may use at most 128 MiB of HBM per device.

v0:
```python
import jax
import jax.numpy as jnp
from jax import lax
from jax.sharding import PartitionSpec as P

HEADS = 16
HD = 64
norm_eps = 1e-05


def shifted(value, axis, steps):
    count = lax.axis_size(axis)
    initial, last = (max(0, -steps), min(count, count - steps))
    return lax.ppermute(value, axis, [(source, source + steps) for source in range(initial, last)])


def gelu_tanh(pre_act):
    return (
        0.5
        * pre_act
        * (1.0 + jnp.tanh(0.7978845608028654 * (pre_act + 0.044715 * pre_act * pre_act * pre_act)))
    )


def norm_fwd(values, gain, shift):
    centred = values - jnp.mean(values, axis=-1, keepdims=True)
    inv_std = lax.rsqrt(jnp.mean(centred * centred, axis=-1, keepdims=True) + norm_eps)
    normed = centred * inv_std
    return (normed * gain + shift, normed, inv_std)


def norm_back(grad_norm, normed, inv_std, gain):
    scaled = grad_norm * gain
    return inv_std * (
        scaled
        - jnp.mean(scaled, axis=-1, keepdims=True)
        - normed * jnp.mean(scaled * normed, axis=-1, keepdims=True)
    )


def rows_product(source, weight, form):
    return jnp.einsum(form, source, weight, preferred_element_type=jnp.float32)


def local(
    section_in,
    lengths,
    qkv_weight,
    qv_bias,
    out_weight,
    up_weight,
    up_bias,
    down_weight,
    norm_gains,
    row_biases,
):
    section_index = lax.axis_index("pipe")
    tensor_index = lax.axis_index("tensor")
    tensor_size = lax.axis_size("tensor")
    groups = section_in.shape[1]
    seq_len = section_in.shape[3]
    model_width = section_in.shape[4]
    total_rows = tensor_size * seq_len
    qkv_w = qkv_weight[0]
    qv_b = qv_bias[0]
    out_w = out_weight[0]
    up_w = up_weight[0]
    up_b = up_bias[0].astype(jnp.float32)
    down_w = down_weight[0]
    gains = norm_gains[0]
    shifts = row_biases[0]
    local_width = qkv_w.shape[2]
    heads_dev = local_width // HD
    head_ids = tensor_index * heads_dev + jnp.arange(heads_dev) + 1
    slopes = 2.0 ** (-8.0 * head_ids.astype(jnp.float32) / HEADS)
    offsets = (jnp.arange(seq_len)[:, None] - jnp.arange(seq_len)[None, :]).astype(jnp.float32)
    key_pos = jnp.arange(seq_len)
    bias_three = jnp.stack([qv_b[0], jnp.zeros_like(qv_b[0]), qv_b[1]]).astype(jnp.float32)[
        :, None, :
    ]
    inputs_all = section_in[0, :, 0]

    def split_heads(block):
        return block.reshape(tensor_size, seq_len, heads_dev, HD)

    def masked_scores(projected, seq_lengths):
        scores = (
            jnp.einsum(
                "bqhd,bkhd->bhqk",
                split_heads(projected[0]),
                split_heads(projected[1]),
                preferred_element_type=jnp.float32,
            )
            * 0.125
            - slopes[None, :, None, None] * offsets
        )
        allowed = (offsets >= 0)[None, None] & (
            key_pos[None, None, None, :] < seq_lengths[:, None, None, None]
        )
        return jnp.where(allowed, scores, -jnp.inf)

    def layer_forward(layer_in, seq_lengths):
        layer_wide = layer_in.astype(jnp.float32)
        attn_f, _, _ = norm_fwd(layer_wide, gains[0], shifts[0])
        attn_full = lax.all_gather(attn_f.astype(jnp.bfloat16), "tensor", axis=0, tiled=True)
        projected = (
            jnp.einsum("rd,cdw->crw", attn_full, qkv_w, preferred_element_type=jnp.float32)
            + bias_three
        ).astype(jnp.bfloat16)
        scores = masked_scores(projected, seq_lengths)
        top_score = jnp.max(scores, axis=-1, keepdims=True)
        exp_scores = jnp.exp(scores - top_score)
        totals = jnp.sum(exp_scores, axis=-1, keepdims=True)
        att_prob = (exp_scores / totals).astype(jnp.bfloat16)
        log_total = top_score + jnp.log(totals)
        context = (
            jnp.einsum(
                "bhqk,bkhd->bqhd",
                att_prob,
                split_heads(projected[2]),
                preferred_element_type=jnp.float32,
            )
            .reshape(total_rows, local_width)
            .astype(jnp.bfloat16)
        )
        attn_out = lax.psum_scatter(
            rows_product(context, out_w, "rw,wd->rd"), "tensor", scatter_dimension=0, tiled=True
        )
        residual = layer_wide + attn_out + shifts[1]
        mlp_f, _, _ = norm_fwd(residual, gains[1], shifts[2])
        mlp_full = lax.all_gather(mlp_f.astype(jnp.bfloat16), "tensor", axis=0, tiled=True)
        pre_gelu = jnp.dot(mlp_full, up_w, preferred_element_type=jnp.float32) + up_b
        activated = gelu_tanh(pre_gelu).astype(jnp.bfloat16)
        mlp_out = lax.psum_scatter(
            rows_product(activated, down_w, "rf,fd->rd"), "tensor", scatter_dimension=0, tiled=True
        )
        layer_out = residual + mlp_out + shifts[3]
        saved = (layer_in, projected, log_total, context, residual, pre_gelu, activated)
        return (layer_out, saved)

    def layer_backward(grad_out, saved, seq_lengths):
        layer_in, projected, log_total, context, residual, pre_gelu, activated = saved[:7]
        attn_f, attn_norm, attn_inv = norm_fwd(layer_in.astype(jnp.float32), gains[0], shifts[0])
        mlp_f, mlp_norm, mlp_inv = norm_fwd(residual, gains[1], shifts[2])
        mlp_full = lax.all_gather(mlp_f.astype(jnp.bfloat16), "tensor", axis=0, tiled=True)
        attn_full = lax.all_gather(attn_f.astype(jnp.bfloat16), "tensor", axis=0, tiled=True)
        grad_full = lax.all_gather(grad_out.astype(jnp.bfloat16), "tensor", axis=0, tiled=True)
        grad_down = jnp.einsum(
            "rf,rd->fd", activated, grad_full, preferred_element_type=jnp.float32
        )
        grad_act = jnp.einsum("rd,fd->rf", grad_full, down_w, preferred_element_type=jnp.float32)
        _, pull_back = jax.vjp(gelu_tanh, pre_gelu)
        grad_pre = pull_back(grad_act)[0]
        grad_pre_half = grad_pre.astype(jnp.bfloat16)
        grad_up = jnp.einsum(
            "rd,rf->df", mlp_full, grad_pre_half, preferred_element_type=jnp.float32
        )
        grad_mlp = lax.psum_scatter(
            rows_product(grad_pre_half, up_w, "rf,df->rd"),
            "tensor",
            scatter_dimension=0,
            tiled=True,
        )
        grad_resid = grad_out + norm_back(grad_mlp, mlp_norm, mlp_inv, gains[1])
        resid_full = lax.all_gather(grad_resid.astype(jnp.bfloat16), "tensor", axis=0, tiled=True)
        grad_outw = jnp.einsum("rw,rd->wd", context, resid_full, preferred_element_type=jnp.float32)
        grad_context = split_heads(
            jnp.einsum("rd,wd->rw", resid_full, out_w, preferred_element_type=jnp.float32).astype(
                jnp.bfloat16
            )
        )
        queries = split_heads(projected[0])
        keys_all = split_heads(projected[1])
        values_all = split_heads(projected[2])
        att_prob = jnp.exp(masked_scores(projected, seq_lengths) - log_total)
        grad_prob = jnp.einsum(
            "bqhd,bkhd->bhqk", grad_context, values_all, preferred_element_type=jnp.float32
        )
        grad_values = jnp.einsum(
            "bhqk,bqhd->bkhd",
            att_prob.astype(jnp.bfloat16),
            grad_context,
            preferred_element_type=jnp.float32,
        )
        row_delta = jnp.sum(att_prob * grad_prob, axis=-1, keepdims=True)
        grad_scores = (att_prob * (grad_prob - row_delta) * 0.125).astype(jnp.bfloat16)
        grad_queries = jnp.einsum(
            "bhqk,bkhd->bqhd", grad_scores, keys_all, preferred_element_type=jnp.float32
        )
        grad_keys = jnp.einsum(
            "bhqk,bqhd->bkhd", grad_scores, queries, preferred_element_type=jnp.float32
        )
        grad_proj = jnp.stack([grad_queries, grad_keys, grad_values]).reshape(
            3, total_rows, local_width
        )
        grad_bias = jnp.stack([jnp.sum(grad_proj[0], axis=0), jnp.sum(grad_proj[2], axis=0)])
        proj_half = grad_proj.astype(jnp.bfloat16)
        grad_qkv = jnp.einsum(
            "rd,crw->cdw", attn_full, proj_half, preferred_element_type=jnp.float32
        )
        grad_attn = lax.psum_scatter(
            rows_product(proj_half, qkv_w, "crw,cdw->rd"), "tensor", scatter_dimension=0, tiled=True
        )
        grad_in = grad_resid + norm_back(grad_attn, attn_norm, attn_inv, gains[0])
        grad_gains = jnp.stack(
            [jnp.sum(grad_attn * attn_norm, axis=0), jnp.sum(grad_mlp * mlp_norm, axis=0)]
        )
        grad_shifts = jnp.stack(
            [
                jnp.sum(grad_attn, axis=0),
                jnp.sum(grad_resid, axis=0),
                jnp.sum(grad_mlp, axis=0),
                jnp.sum(grad_out, axis=0),
            ]
        )
        return (
            grad_in,
            (
                grad_qkv,
                grad_bias,
                grad_outw,
                grad_up,
                jnp.sum(grad_pre, axis=0),
                grad_down,
                grad_gains,
                grad_shifts,
            ),
        )

    def forward_tick(received, tick_index):
        own_at = jnp.minimum(tick_index, groups - 1)
        batch_at = jnp.clip(tick_index - section_index, 0, groups - 1)
        own_in = lax.dynamic_index_in_dim(inputs_all, own_at, 0, keepdims=False)
        layer_in = jnp.where(section_index == 0, own_in, received)
        seq_lengths = lax.dynamic_index_in_dim(lengths, batch_at, 0, keepdims=False)
        layer_out, saved = layer_forward(layer_in, seq_lengths)
        passed = shifted(layer_out.astype(jnp.bfloat16), "pipe", 1)
        return (passed, (layer_out, saved))

    start_rows = jnp.zeros((seq_len, model_width), jnp.bfloat16)
    _, (outputs_all, saves_all) = lax.scan(forward_tick, start_rows, jnp.arange(groups + 1))
    zero_sums = (
        jnp.zeros(qkv_w.shape, jnp.float32),
        jnp.zeros(qv_b.shape, jnp.float32),
        jnp.zeros(out_w.shape, jnp.float32),
        jnp.zeros(up_w.shape, jnp.float32),
        jnp.zeros(up_b.shape, jnp.float32),
        jnp.zeros(down_w.shape, jnp.float32),
        jnp.zeros((2, model_width), jnp.float32),
        jnp.zeros((4, model_width), jnp.float32),
    )

    def backward_tick(carry, tick_index):
        received, running = carry
        source_at = jnp.clip(tick_index + 2 * section_index - 1, 0, groups)
        batch_at = jnp.clip(tick_index + section_index - 1, 0, groups - 1)
        saved = jax.tree.map(
            lambda stacked: lax.dynamic_index_in_dim(stacked, source_at, 0, keepdims=False),
            saves_all,
        )
        own_cot = lax.dynamic_index_in_dim(
            inputs_all, jnp.minimum(tick_index, groups - 1), 0, keepdims=False
        ).astype(jnp.float32)
        live_cot = jnp.where(tick_index < groups, own_cot, jnp.zeros_like(own_cot))
        grad_out = jnp.where(section_index == 1, live_cot, received.astype(jnp.float32))
        seq_lengths = lax.dynamic_index_in_dim(lengths, batch_at, 0, keepdims=False)
        grad_in, terms = layer_backward(grad_out, saved, seq_lengths)
        passed = shifted(grad_in.astype(jnp.bfloat16), "pipe", -1)
        running = tuple((total + term for total, term in zip(running, terms)))
        return ((passed, running), grad_in)

    (_, sums), grads_all = lax.scan(backward_tick, (start_rows, zero_sums), jnp.arange(groups + 1))
    weight_sums = lax.psum((sums[0], sums[1], sums[2], sums[3], sums[4], sums[5]), "dp")
    vector_sums = lax.psum((sums[6], sums[7]), ("tensor", "dp"))
    section_out = jnp.where(section_index == 0, grads_all[1:], outputs_all[1:])[None, :, None]
    return (
        section_out,
        weight_sums[0][None],
        weight_sums[1][None],
        weight_sums[2][None],
        weight_sums[3][None],
        weight_sums[4][None],
        weight_sums[5][None],
        vector_sums[0][None],
        vector_sums[1][None],
    )


def solution(mesh):
    in_specs = (
        P("pipe", "dp", "tensor", None, None),
        P("dp", None),
        P("pipe", None, None, "tensor"),
        P("pipe", None, "tensor"),
        P("pipe", "tensor", None),
        P("pipe", None, "tensor"),
        P("pipe", "tensor"),
        P("pipe", "tensor", None),
        P("pipe", None, None),
        P("pipe", None, None),
    )
    out_specs = (
        P("pipe", "dp", "tensor", None, None),
        P("pipe", None, None, "tensor"),
        P("pipe", None, "tensor"),
        P("pipe", "tensor", None),
        P("pipe", None, "tensor"),
        P("pipe", "tensor"),
        P("pipe", "tensor", None),
        P("pipe", None, None),
        P("pipe", None, None),
    )
    return jax.shard_map(local, mesh=mesh, in_specs=in_specs, out_specs=out_specs, check_vma=False)
```

profile of v0, /device:TPU:0, one launch (start us, length us, event | category | flops | bytes accessed | tf_op | source)
XLA Modules:
  0.0 1544.7 jit_solution(1438076503732215553)
XLA Ops:
  13.6 189.5 %while.63 = (s32[]{:T(128)}, bf16[128,1024]{1,0:T(8,128)(2,1)}, f32[2,128,1024]{2,1,0:T(8,128)}, bf16[2,128,1024]{2,1,0:T(8,128)(2,1)}, bf16[2,3,256,512]{3,2,1,...) while((s32[]{:T(128)}, bf16[128,1024]{1,0:T(8,128)(2,1)}, ...), condition=%wide.region_9.10_spmd.clone.clone, body=%wide.region_0.9_spmd.clone.clone.sunk | while | flops 2227026432 | bytes 96496376 | solution.py:241
  16.5 9.5 all_gather.54
  38.9 25.6 %reduce-scatter.5.cloned.1.call-done = f32[128,1024]{1,0:T(8,128)} async-done(((f32[256,1024]{1,0:T(8,128)}), f32[128,1024]{1,0:T(8,128)}) %reduce-scatter.5.cloned.1.call-update) | async-done | bytes 524304 | tf_op jit(solution)/shard_map/while/body/eval_jaxpr/reduce_scatter | solution.py:126
  67.0 8.8 all_gather.55
  83.3 20.7 %reduce-scatter.7.cloned.1.call-done = f32[128,1024]{1,0:T(8,128)} async-done(((f32[256,1024]{1,0:T(8,128)}), f32[128,1024]{1,0:T(8,128)}) %reduce-scatter.7.cloned.1.call-update) | async-done | bytes 524304 | tf_op jit(solution)/shard_map/while/body/eval_jaxpr/reduce_scatter | solution.py:134
  112.4 8.8 all_gather.54
  134.1 23.9 %reduce-scatter.5.cloned.1.call-done = f32[128,1024]{1,0:T(8,128)} async-done(((f32[256,1024]{1,0:T(8,128)}), f32[128,1024]{1,0:T(8,128)}) %reduce-scatter.5.cloned.1.call-update) | async-done | bytes 524304 | tf_op jit(solution)/shard_map/while/body/eval_jaxpr/reduce_scatter | solution.py:126
  160.5 8.8 all_gather.55
  176.8 20.7 %reduce-scatter.7.cloned.1.call-done = f32[128,1024]{1,0:T(8,128)} async-done(((f32[256,1024]{1,0:T(8,128)}), f32[128,1024]{1,0:T(8,128)}) %reduce-scatter.7.cloned.1.call-update) | async-done | bytes 524304 | tf_op jit(solution)/shard_map/while/body/eval_jaxpr/reduce_scatter | solution.py:134
  205.5 253.4 %while.64 = (s32[]{:T(128)}, bf16[128,1024]{1,0:T(8,128)(2,1)}, f32[3,1024,512]{1,2,0:T(8,128)}, f32[2,512]{1,0:T(2,128)}, f32[512,1024]{1,0:T(8,128)}, /*index=...) while((s32[]{:T(128)}, bf16[128,1024]{1,0:T(8,128)(2,1)}, ...), condition=%wide.region_31.32_spmd.clone.clone, body=%wide.region_10.31_spmd.clone.clone.sunk | while | flops 4491193856 | bytes 120951592 | solution.py:272
  209.1 7.9 all_gather.56
  251.9 8.7 all_gather.57
  289.8 11.6 all_gather.59
  315.1 9.0 all_gather.58
  332.1 9.5 all_gather.56
  376.7 8.7 all_gather.57
  410.4 5.3 select_add_fusion.11
  415.9 13.3 all_gather.59
  442.7 9.0 all_gather.58
  451.7 6.6 bitcast_add_fusion.2
  458.9 6.6 copy.63
  466.2 104.3 %all-reduce.1 = (f32[1,2,512]{2,1,0:T(2,128)}, f32[1,1024]{1,0:T(1,128)}) all-reduce(f32[1,2,512]{2,1,0:T(2,128)S(1)} %bitcast.394, f32[1,1024]{1,0:T(1,128)S(1)} %bitcast.393), channel_id=1, replica_groups=mesh['pipe'=2,'tensor'=2,'dp'=32] {'dp'}, use_global_device_ids=true, to_apply=%region_33.34 | all-reduce | flops 2048 | bytes 16384 | tf_op jit(solution)/shard_map/psum | solution.py:273
  570.6 950.9 %all-reduce = (f32[1,2,1024]{2,1,0:T(2,128)}, f32[1,4,1024]{2,1,0:T(4,128)}) all-reduce(f32[1,2,1024]{2,1,0:T(2,128)S(1)} %bitcast.392, f32[1,4,1024]{2,1,0:T(4,128)S(1)} %bitcast.377), channel_id=1, replica_groups=mesh['pipe'=2,'tensor'=2,'dp'=32] {'tensor','dp'}, use_global_device_ids=true, to_apply=%region_38.39 | all-reduce | flops 6144 | bytes 49152 | tf_op jit(solution)/shard_map/psum | solution.py:274
  1522.3 6.3 copy.215
  (415 shorter events, 240.8 us)
Async XLA Ops:
  13.6 50.9 %reduce-scatter.5.cloned.1.call-start = ((), (), s32[]{:S(2)}) async-start(), calls=%async_computation.5 | async-start | bytes 1572864 | tf_op jit(solution)/shard_map/while/body/eval_jaxpr/reduce_scatter | solution.py:126
  13.7 12.3 copy-start.15
  13.7 12.3 copy-start.41
  38.9 65.1 %reduce-scatter.7.cloned.1.call-start = ((), (), s32[]{:S(2)}) async-start(), calls=%async_computation.6 | async-start | bytes 1572864 | tf_op jit(solution)/shard_map/while/body/eval_jaxpr/reduce_scatter | solution.py:134
  80.9 28.6 %copy-start.39 = (f32[2,2,8,128,1]{3,2,1,4,0:T(8,128)}, f32[2,2,8,128,1]{3,2,1,4,0:T(8,128)S(1)}, u32[]{:S(2)}) copy-start(f32[2,2,8,128,1]{3,2,1,4,0:T(8,128)S(1)} %bitcast_dynamic-update-slice_fusion.21) | copy-start | bytes 49156 | tf_op jit(solution)/shard_map/while
  105.1 4.4 collective-permute-start
  109.5 48.5 %reduce-scatter.5.cloned.1.call-start = ((), (), s32[]{:S(2)}) async-start(), calls=%async_computation.5 | async-start | bytes 1572864 | tf_op jit(solution)/shard_map/while/body/eval_jaxpr/reduce_scatter | solution.py:126
  134.0 63.5 %reduce-scatter.7.cloned.1.call-start = ((), (), s32[]{:S(2)}) async-start(), calls=%async_computation.6 | async-start | bytes 1572864 | tf_op jit(solution)/shard_map/while/body/eval_jaxpr/reduce_scatter | solution.py:134
  174.5 28.6 %copy-start.39 = (f32[2,2,8,128,1]{3,2,1,4,0:T(8,128)}, f32[2,2,8,128,1]{3,2,1,4,0:T(8,128)S(1)}, u32[]{:S(2)}) copy-start(f32[2,2,8,128,1]{3,2,1,4,0:T(8,128)S(1)} %bitcast_dynamic-update-slice_fusion.21) | copy-start | bytes 49156 | tf_op jit(solution)/shard_map/while
  198.6 4.4 collective-permute-start
  205.5 44.1 %copy-start.8 = (bf16[1,128,1024]{2,1,0:T(8,128)(2,1)}, bf16[1,128,1024]{2,1,0:T(8,128)(2,1)S(1)}, u32[]{:S(2)}) copy-start(bf16[1,128,1024]{2,1,0:T(8,128)(2,1)S(1)} %get-tuple-element.1786) | copy-start | bytes 786436 | tf_op jit(solution)/shard_map/while
  205.5 42.1 %reduce-scatter.9.cloned.1.call-start = ((), (), s32[]{:S(2)}) async-start(), calls=%async_computation.7 | async-start | bytes 1572864 | tf_op jit(solution)/shard_map/while/body/eval_jaxpr/reduce_scatter | solution.py:158
  223.6 86.6 %reduce-scatter.11.cloned.1.call-start = ((), (), s32[]{:S(2)}) async-start(), calls=%async_computation.8 | async-start | bytes 1572864 | tf_op jit(solution)/shard_map/while/body/eval_jaxpr/reduce_scatter | solution.py:201
  285.7 15.7 %copy-start.31 = (f32[2,512]{1,0:T(2,128)S(1)}, f32[2,512]{1,0:T(2,128)}, u32[]{:S(2)}) copy-start(f32[2,512]{1,0:T(2,128)} %get-tuple-element.1741) | copy-start | bytes 12292 | tf_op jit(solution)/shard_map/while
  313.9 14.1 collective-permute-start.1
  328.5 45.8 %copy-start.8 = (bf16[1,128,1024]{2,1,0:T(8,128)(2,1)}, bf16[1,128,1024]{2,1,0:T(8,128)(2,1)S(1)}, u32[]{:S(2)}) copy-start(bf16[1,128,1024]{2,1,0:T(8,128)(2,1)S(1)} %get-tuple-element.1786) | copy-start | bytes 786436 | tf_op jit(solution)/shard_map/while
  328.5 43.8 %reduce-scatter.9.cloned.1.call-start = ((), (), s32[]{:S(2)}) async-start(), calls=%async_computation.7 | async-start | bytes 1572864 | tf_op jit(solution)/shard_map/while/body/eval_jaxpr/reduce_scatter | solution.py:158
  348.4 89.4 %reduce-scatter.11.cloned.1.call-start = ((), (), s32[]{:S(2)}) async-start(), calls=%async_computation.8 | async-start | bytes 1572864 | tf_op jit(solution)/shard_map/while/body/eval_jaxpr/reduce_scatter | solution.py:201
  410.4 18.7 %copy-start.31 = (f32[2,512]{1,0:T(2,128)S(1)}, f32[2,512]{1,0:T(2,128)}, u32[]{:S(2)}) copy-start(f32[2,512]{1,0:T(2,128)} %get-tuple-element.1741) | copy-start | bytes 12292 | tf_op jit(solution)/shard_map/while
  441.4 17.0 %collective-permute-start.1 = (bf16[128,1024]{1,0:T(8,128)(2,1)S(1)}, bf16[128,1024]{1,0:T(8,128)(2,1)}, u32[]{:S(2)}, u32[]{:S(2)}) collective-permute-start(bf16[128,1024]{1,0:T(8,128)(2,1)S(1)} %get-tuple-element.1618), channel_id=1, source_target_pairs={{64,0},{65,1},{66,2},{67,3},{68,4},{69,5},{70,6},{71,7},{72,8},{73... | collective-permute-start | bytes 786440 | tf_op jit(solution)/shard_map/while/body/eval_jaxpr/ppermute | solution.py:14
  458.9 1063.4 %all-reduce.5.cloned.1.call-start = ((), (), s32[]{:S(2)}) async-start(), calls=%async_computation.4 | async-start | bytes 33554432 | tf_op jit(solution)/shard_map/psum | solution.py:273
  465.5 105.0 %copy-start.27 = (f32[2,1024]{1,0:T(2,128)S(1)}, f32[2,1024]{1,0:T(2,128)}, u32[]{:S(2)}) copy-start(f32[2,1024]{1,0:T(2,128)} %get-tuple-element.751) | copy-start | bytes 24580
  465.5 1055.9 %copy-start.20 = (f32[2,128,1024]{2,1,0:T(8,128)S(1)}, f32[2,128,1024]{2,1,0:T(8,128)}, u32[]{:S(2)}) copy-start(f32[2,128,1024]{2,1,0:T(8,128)} %get-tuple-element.743) | copy-start | bytes 3145732
  465.5 1055.9 %copy-start.21 = (f32[2,128,1024]{2,1,0:T(8,128)S(1)}, f32[2,128,1024]{2,1,0:T(8,128)}, u32[]{:S(2)}) copy-start(f32[2,128,1024]{2,1,0:T(8,128)} %get-tuple-element.744) | copy-start | bytes 3145732
  (67 other events, 274.7 us)
Sparse Core Ops, SparseCore 0:
  39.0 25.4 reduce-scatter.4
  80.1 23.8 reduce-scatter.6
  134.2 23.7 reduce-scatter.4
  173.7 23.8 reduce-scatter.6
  223.7 23.7 reduce-scatter.8
  284.6 25.6 reduce-scatter.10
  348.5 23.7 reduce-scatter.8
  409.3 26.9 reduce-scatter.10
Sparse Core Ops, SparseCore 1:
  465.6 743.7 all-reduce.4
where the time goes:
time: 1550 us; the launch traced here: 1540 us
  blocking collectives  1170 us (75%)
  waiting for transfers between devices  99.9 us (6%)
  local copies, waits for them, and re-layouts  99 us (6%)
  matrix products  98.1 us (6%)
  other arithmetic  51.6 us (3%)
  between operations  15.6 us (1%)
    psum x1, blocking collectives, local(): vector_sums = lax.psum((sums[6], sums[7]), ('tensor', 'dp'))  951 us
    psum x1, blocking collectives, local(): lax.psum((sums[0], sums[1], sums[2], sums[3], sums[4], sums[5]), 'dp')  104 us
    reduce_scatter x2, waiting for transfers between devices, layer_forward(): lax.psum_scatter(rows_product(context, out_w, 'rw,wd->rd'), 'tensor', sca...  49.5 us
    reduce_scatter x2, waiting for transfers between devices, layer_forward(): lax.psum_scatter(rows_product(activated, down_w, 'rf,fd->rd'), 'tensor',...  41.4 us
    squeeze x18, local copies, waits for them, and re-layouts, split_heads(): return block.reshape(tensor_size, seq_len, heads_dev, HD)  31.4 us
  transfers between devices with their start and end apart: 13, of which 7 were waited for; matrix products, arithmetic and copies ran while one was open for 6% of the time, Pallas kernels for 0%

commit v1 on v0

--- a/solution.py
+++ b/solution.py
@@ -1,3 +1,4 @@
+import functools
 import jax
 import jax.numpy as jnp
 from jax import lax
@@ -6,6 +7,14 @@
 HEADS = 16
 HD = 64
 norm_eps = 1e-05
+
+
+def get_lines(here_x, axis_name, peer_axis):
+    piece_out = lax.psum(here_x, axis_name=axis_name)
+    return lax.psum(piece_out, axis_name=peer_axis)
+
+
+review_sums_all = functools.partial(get_lines, axis_name="tensor", peer_axis="dp")
 
 
 def shifted(value, axis, steps):
@@ -271,7 +280,7 @@
 
     (_, sums), grads_all = lax.scan(backward_tick, (start_rows, zero_sums), jnp.arange(groups + 1))
     weight_sums = lax.psum((sums[0], sums[1], sums[2], sums[3], sums[4], sums[5]), "dp")
-    vector_sums = lax.psum((sums[6], sums[7]), ("tensor", "dp"))
+    vector_sums = review_sums_all((sums[6], sums[7]))
     section_out = jnp.where(section_index == 0, grads_all[1:], outputs_all[1:])[None, :, None]
     return (
         section_out,

time: 1550 us -> 1230 us (0.79)
  blocking collectives: 1170 us -> 315 us
  waiting for transfers between devices: 99.9 us -> 640 us
    psum x1, blocking collectives: 951 us -> 7.03 us  [get_lines(): piece_out = lax.psum(here_x, axis_name=axis_name)]
    psum x1, waiting for transfers between devices: 0.01 us -> 540 us  [local(): lax.psum((sums[0], sums[1], sums[2], sums[3], sums[4], sums[5]), 'dp')]
    psum x1, blocking collectives: 104 us -> 194 us  [local(): lax.psum((sums[0], sums[1], sums[2], sums[3], sums[4], sums[5]), 'dp')]
  transfers between devices with their start and end apart: 13 -> 13, of which waited for: 7 -> 8; matrix products, arithmetic and copies ran while one was open for 6% -> 7% of each run, Pallas kernels for 0% -> 0%
where the time goes in v1:
time: 1230 us
  waiting for transfers between devices  640 us (52%)
  blocking collectives  315 us (26%)
  local copies, waits for them, and re-layouts  99 us (8%)
  matrix products  98.1 us (8%)
  other arithmetic  51.6 us (4%)
  between operations  15.7 us (1%)
    psum x1, waiting for transfers between devices, local(): lax.psum((sums[0], sums[1], sums[2], sums[3], sums[4], sums[5]), 'dp')  540 us
    psum x1, blocking collectives, local(): lax.psum((sums[0], sums[1], sums[2], sums[3], sums[4], sums[5]), 'dp')  194 us
    reduce_scatter x2, waiting for transfers between devices, layer_forward(): lax.psum_scatter(rows_product(context, out_w, 'rw,wd->rd'), 'tensor', sca...  49.5 us
    reduce_scatter x2, waiting for transfers between devices, layer_forward(): lax.psum_scatter(rows_product(activated, down_w, 'rf,fd->rd'), 'tensor',...  41.4 us
    squeeze x18, local copies, waits for them, and re-layouts, split_heads(): return block.reshape(tensor_size, seq_len, heads_dev, HD)  31.4 us
    all_gather x2, blocking collectives, layer_backward(): lax.all_gather(mlp_f.astype(jnp.bfloat16), 'tensor', axis=0, tiled=True)  24.9 us
  transfers between devices with their start and end apart: 13, of which 8 were waited for; matrix products, arithmetic and copies ran while one was open for 7% of the time, Pallas kernels for 0%

profile of v1, /device:TPU:0, one launch (start us, length us, event | category | flops | bytes accessed | tf_op | source)
XLA Modules:
  0.0 1230.5 jit_solution(11006682290865692937)
XLA Ops:
  13.6 189.5 %while.63 = (s32[]{:T(128)}, bf16[128,1024]{1,0:T(8,128)(2,1)}, f32[2,128,1024]{2,1,0:T(8,128)}, bf16[2,128,1024]{2,1,0:T(8,128)(2,1)}, bf16[2,3,256,512]{3,2,1,...) while((s32[]{:T(128)}, bf16[128,1024]{1,0:T(8,128)(2,1)}, ...), condition=%wide.region_9.10_spmd.clone.clone, body=%wide.region_0.9_spmd.clone.clone.sunk | while | flops 2227026432 | bytes 96496376 | solution.py:250
  16.5 9.5 all_gather.54
  38.9 25.6 %reduce-scatter.5.cloned.1.call-done = f32[128,1024]{1,0:T(8,128)} async-done(((f32[256,1024]{1,0:T(8,128)}), f32[128,1024]{1,0:T(8,128)}) %reduce-scatter.5.cloned.1.call-update) | async-done | bytes 524304 | tf_op jit(solution)/shard_map/while/body/eval_jaxpr/reduce_scatter | solution.py:135
  67.0 8.8 all_gather.55
  83.3 20.7 %reduce-scatter.7.cloned.1.call-done = f32[128,1024]{1,0:T(8,128)} async-done(((f32[256,1024]{1,0:T(8,128)}), f32[128,1024]{1,0:T(8,128)}) %reduce-scatter.7.cloned.1.call-update) | async-done | bytes 524304 | tf_op jit(solution)/shard_map/while/body/eval_jaxpr/reduce_scatter | solution.py:143
  112.4 8.8 all_gather.54
  134.1 23.9 %reduce-scatter.5.cloned.1.call-done = f32[128,1024]{1,0:T(8,128)} async-done(((f32[256,1024]{1,0:T(8,128)}), f32[128,1024]{1,0:T(8,128)}) %reduce-scatter.5.cloned.1.call-update) | async-done | bytes 524304 | tf_op jit(solution)/shard_map/while/body/eval_jaxpr/reduce_scatter | solution.py:135
  160.5 8.8 all_gather.55
  176.8 20.7 %reduce-scatter.7.cloned.1.call-done = f32[128,1024]{1,0:T(8,128)} async-done(((f32[256,1024]{1,0:T(8,128)}), f32[128,1024]{1,0:T(8,128)}) %reduce-scatter.7.cloned.1.call-update) | async-done | bytes 524304 | tf_op jit(solution)/shard_map/while/body/eval_jaxpr/reduce_scatter | solution.py:143
  205.5 253.4 %while.64 = (s32[]{:T(128)}, bf16[128,1024]{1,0:T(8,128)(2,1)}, f32[3,1024,512]{1,2,0:T(8,128)}, f32[2,512]{1,0:T(2,128)}, f32[512,1024]{1,0:T(8,128)}, /*index=...) while((s32[]{:T(128)}, bf16[128,1024]{1,0:T(8,128)(2,1)}, ...), condition=%wide.region_31.32_spmd.clone.clone, body=%wide.region_10.31_spmd.clone.clone.sunk | while | flops 4491193856 | bytes 120951592 | solution.py:281
  209.1 7.9 all_gather.56
  251.9 8.7 all_gather.57
  289.8 11.6 all_gather.59
  315.1 9.0 all_gather.58
  332.1 9.5 all_gather.56
  376.7 8.7 all_gather.57
  415.9 13.3 %all_gather.59 = bf16[256,1024]{1,0:T(8,128)(2,1)S(1)} all-gather(bf16[128,1024]{1,0:T(8,128)(2,1)} %get-tuple-element.1624), channel_id=1, replica_groups=mesh['pipe'=2,'tensor'=2,'dp'=32] {'tensor'}, dimensions={0}, use_global_device_ids=true | all-gather | bytes 786432 | tf_op jit(solution)/shard_map/while/body/eval_jaxpr/all_gather | solution.py:154
  442.7 9.0 all_gather.58
  451.7 6.6 bitcast_add_fusion.2
  458.9 6.6 copy.63
  466.2 7.0 all-reduce.2
  473.3 193.9 %all-reduce = (f32[1,2,512]{2,1,0:T(2,128)}, f32[1,1024]{1,0:T(1,128)}, f32[1,2,1024]{2,1,0:T(2,128)}, f32[1,4,1024]{2,1,0:T(4,128)}) all-reduce(f32[1,2,512]{2,1,0:T(2,128)S(1)} %bitcast.392, f32[1,1024]{1,0:T(1,128)S(1)} %bitcast.391, f32[1,2,1024]{2,1,0:T(2,128)S(1)} %bitcast.395, ...), channel_id=1, replica_groups=mesh['pipe'=2,'tensor'=2,'dp'=32] {'dp'}, use_global_device_ids=true, to_apply=%region_33.34 | all-reduce | flops 8192 | bytes 65536 | tf_op jit(solution)/shard_map/psum | solution.py:282
  668.0 540.0 %all-reduce.5.cloned.1.call-done = (f32[1,3,1024,512]{3,2,1,0:T(8,128)}, f32[1,512,1024]{2,1,0:T(8,128)}, f32[1,1024,1024]{2,1,0:T(8,128)}, f32[1,1024,1024]{2,1,0:T(8,128)}) async-done(((f32[1,3,1024,512]{3,2,1,0:T(8,128)}, f32[1,512,1024]{2,1,0:T(8,128)}, f32[1,1024,1024]{2,1,0:T(8,128)}, f32[1,1024,1024]{2,1,0:T(8,128)}), (f32[1,3,1024,512]{3,2,1,0:T(8,128)}, f32[1,512,1024]{2,1,0:T(8,128)}, ...) | async-done | bytes 16777232 | tf_op jit(solution)/shard_map/psum | solution.py:282
  1208.0 6.3 copy.215
  (415 shorter events, 246.0 us)
Async XLA Ops:
  13.6 50.9 %reduce-scatter.5.cloned.1.call-start = ((), (), s32[]{:S(2)}) async-start(), calls=%async_computation.5 | async-start | bytes 1572864 | tf_op jit(solution)/shard_map/while/body/eval_jaxpr/reduce_scatter | solution.py:135
  13.7 12.3 %copy-start.15 = (bf16[2,3,256,512]{3,2,1,0:T(8,128)(2,1)S(1)}, bf16[2,3,256,512]{3,2,1,0:T(8,128)(2,1)}, u32[]{:S(2)}) copy-start(bf16[2,3,256,512]{3,2,1,0:T(8,128)(2,1)} %get-tuple-element.1661) | copy-start | bytes 4718596 | tf_op jit(solution)/shard_map/while
  13.7 12.3 %copy-start.41 = (f32[3,1,512]{2,0,1:T(4,128)S(1)}, f32[3,1,512]{2,0,1:T(4,128)}, u32[]{:S(2)}) copy-start(f32[3,1,512]{2,0,1:T(4,128)} %get-tuple-element.1696) | copy-start | bytes 18436 | tf_op jit(solution)/shard_map/while
  38.9 65.1 %reduce-scatter.7.cloned.1.call-start = ((), (), s32[]{:S(2)}) async-start(), calls=%async_computation.6 | async-start | bytes 1572864 | tf_op jit(solution)/shard_map/while/body/eval_jaxpr/reduce_scatter | solution.py:143
  80.9 28.6 %copy-start.39 = (f32[2,2,8,128,1]{3,2,1,4,0:T(8,128)}, f32[2,2,8,128,1]{3,2,1,4,0:T(8,128)S(1)}, u32[]{:S(2)}) copy-start(f32[2,2,8,128,1]{3,2,1,4,0:T(8,128)S(1)} %bitcast_dynamic-update-slice_fusion.21) | copy-start | bytes 49156 | tf_op jit(solution)/shard_map/while
  105.1 4.4 collective-permute-start
  109.5 48.5 %reduce-scatter.5.cloned.1.call-start = ((), (), s32[]{:S(2)}) async-start(), calls=%async_computation.5 | async-start | bytes 1572864 | tf_op jit(solution)/shard_map/while/body/eval_jaxpr/reduce_scatter | solution.py:135
  109.6 11.6 copy-start.15
  134.0 63.5 %reduce-scatter.7.cloned.1.call-start = ((), (), s32[]{:S(2)}) async-start(), calls=%async_computation.6 | async-start | bytes 1572864 | tf_op jit(solution)/shard_map/while/body/eval_jaxpr/reduce_scatter | solution.py:143
  174.5 28.6 %copy-start.39 = (f32[2,2,8,128,1]{3,2,1,4,0:T(8,128)}, f32[2,2,8,128,1]{3,2,1,4,0:T(8,128)S(1)}, u32[]{:S(2)}) copy-start(f32[2,2,8,128,1]{3,2,1,4,0:T(8,128)S(1)} %bitcast_dynamic-update-slice_fusion.21) | copy-start | bytes 49156 | tf_op jit(solution)/shard_map/while
  198.6 4.4 collective-permute-start
  205.5 44.1 %copy-start.8 = (bf16[1,128,1024]{2,1,0:T(8,128)(2,1)}, bf16[1,128,1024]{2,1,0:T(8,128)(2,1)S(1)}, u32[]{:S(2)}) copy-start(bf16[1,128,1024]{2,1,0:T(8,128)(2,1)S(1)} %get-tuple-element.1788) | copy-start | bytes 786436 | tf_op jit(solution)/shard_map/while
  205.5 42.1 %reduce-scatter.9.cloned.1.call-start = ((), (), s32[]{:S(2)}) async-start(), calls=%async_computation.7 | async-start | bytes 1572864 | tf_op jit(solution)/shard_map/while/body/eval_jaxpr/reduce_scatter | solution.py:167
  223.6 86.6 %reduce-scatter.11.cloned.1.call-start = ((), (), s32[]{:S(2)}) async-start(), calls=%async_computation.8 | async-start | bytes 1572864 | tf_op jit(solution)/shard_map/while/body/eval_jaxpr/reduce_scatter | solution.py:210
  285.7 15.7 %copy-start.31 = (f32[2,512]{1,0:T(2,128)S(1)}, f32[2,512]{1,0:T(2,128)}, u32[]{:S(2)}) copy-start(f32[2,512]{1,0:T(2,128)} %get-tuple-element.1743) | copy-start | bytes 12292 | tf_op jit(solution)/shard_map/while
  313.9 14.1 %collective-permute-start.1 = (bf16[128,1024]{1,0:T(8,128)(2,1)S(1)}, bf16[128,1024]{1,0:T(8,128)(2,1)}, u32[]{:S(2)}, u32[]{:S(2)}) collective-permute-start(bf16[128,1024]{1,0:T(8,128)(2,1)S(1)} %get-tuple-element.1620), channel_id=1, source_target_pairs={{64,0},{65,1},{66,2},{67,3},{68,4},{69,5},{70,6},{71,7},{72,8},{73... | collective-permute-start | bytes 786440 | tf_op jit(solution)/shard_map/while/body/eval_jaxpr/ppermute | solution.py:23
  328.5 45.8 %copy-start.8 = (bf16[1,128,1024]{2,1,0:T(8,128)(2,1)}, bf16[1,128,1024]{2,1,0:T(8,128)(2,1)S(1)}, u32[]{:S(2)}) copy-start(bf16[1,128,1024]{2,1,0:T(8,128)(2,1)S(1)} %get-tuple-element.1788) | copy-start | bytes 786436 | tf_op jit(solution)/shard_map/while
  328.5 43.8 %reduce-scatter.9.cloned.1.call-start = ((), (), s32[]{:S(2)}) async-start(), calls=%async_computation.7 | async-start | bytes 1572864 | tf_op jit(solution)/shard_map/while/body/eval_jaxpr/reduce_scatter | solution.py:167
  348.4 89.4 %reduce-scatter.11.cloned.1.call-start = ((), (), s32[]{:S(2)}) async-start(), calls=%async_computation.8 | async-start | bytes 1572864 | tf_op jit(solution)/shard_map/while/body/eval_jaxpr/reduce_scatter | solution.py:210
  410.4 18.7 %copy-start.31 = (f32[2,512]{1,0:T(2,128)S(1)}, f32[2,512]{1,0:T(2,128)}, u32[]{:S(2)}) copy-start(f32[2,512]{1,0:T(2,128)} %get-tuple-element.1743) | copy-start | bytes 12292 | tf_op jit(solution)/shard_map/while
  441.4 17.0 %collective-permute-start.1 = (bf16[128,1024]{1,0:T(8,128)(2,1)S(1)}, bf16[128,1024]{1,0:T(8,128)(2,1)}, u32[]{:S(2)}, u32[]{:S(2)}) collective-permute-start(bf16[128,1024]{1,0:T(8,128)(2,1)S(1)} %get-tuple-element.1620), channel_id=1, source_target_pairs={{64,0},{65,1},{66,2},{67,3},{68,4},{69,5},{70,6},{71,7},{72,8},{73... | collective-permute-start | bytes 786440 | tf_op jit(solution)/shard_map/while/body/eval_jaxpr/ppermute | solution.py:23
  458.9 749.1 %all-reduce.5.cloned.1.call-start = ((), (), s32[]{:S(2)}) async-start(), calls=%async_computation.4 | async-start | bytes 33554432 | tf_op jit(solution)/shard_map/psum | solution.py:282
  465.5 201.6 %copy-start.20 = (f32[2,128,1024]{2,1,0:T(8,128)S(1)}, f32[2,128,1024]{2,1,0:T(8,128)}, u32[]{:S(2)}) copy-start(f32[2,128,1024]{2,1,0:T(8,128)} %get-tuple-element.743) | copy-start | bytes 3145732
  465.5 201.6 %copy-start.21 = (f32[2,128,1024]{2,1,0:T(8,128)S(1)}, f32[2,128,1024]{2,1,0:T(8,128)}, u32[]{:S(2)}) copy-start(f32[2,128,1024]{2,1,0:T(8,128)} %get-tuple-element.744) | copy-start | bytes 3145732
  (67 other events, 277.9 us)
Sparse Core Ops, SparseCore 0:
  39.0 25.4 reduce-scatter.4
  80.1 23.8 reduce-scatter.6
  134.2 23.7 reduce-scatter.4
  173.7 23.8 reduce-scatter.6
  223.7 23.7 reduce-scatter.8
  284.6 25.6 reduce-scatter.10
  348.5 23.7 reduce-scatter.8
  409.3 26.9 reduce-scatter.10
Sparse Core Ops, SparseCore 1:
  465.6 742.3 all-reduce.4
